TPU v7x, 32 devices: a whole 2x2x4 slice. The times are simulated.
32 devices in a mesh: section: 8 (over y, x, core), shard: 4 (over z).
Axes of the slice: x: 2, y: 2, z: 4, core: 2. Of those that a mesh axis runs over, the one named last changes fastest.
Arguments:
- kept_slab: bfloat16 [131072, 768], P(('section', 'shard')), may hold values from -1 to 1, as said below
- new_rows: bfloat16 [4, 256, 768], P(None, ('section', 'shard')), may hold values from -1 to 1, as said below
- append_mask: int32 [4, 256], P(None, ('section', 'shard')), may hold values 0 or 1
Outputs:
- maxima: float32 [4, 256], P(None, ('section', 'shard'))
Inputs may be any that keep to these rules, and one draw needn't show every extreme that they name: `kept_slab`: every row has unit Euclidean length up to bfloat16 rounding. `new_rows`: every row has unit Euclidean length up to bfloat16 rounding.
All inputs are finite; a program needn't handle non-finite values. No bound on the sum of `append_mask` on one device may be relied on, other than what follows from the above.
Results may differ from a plain program's by a relative error of at most 0.0003.
Values may be sent and summed in bfloat16 or wider, within the bound.
No kernel may reach another device: no remote copies, remote signals or barrier semaphores. Data moves between devices by JAX's collectives and lax.ppermute only.
A program may use at most 64 MiB of HBM per device.

v0:
```python
import functools

import jax
import jax.numpy as jnp
from jax import lax
from jax.experimental import pallas as pl
from jax.experimental.pallas import tpu as pltpu
from jax.sharding import PartitionSpec as P

AXES = ("section", "shard")
LANES = 128
CHUNK_ROWS = 256
JOIN_FLOPS = 4_000_000_000
NONE_YET = -3.0


def partner_mask(mesh):
    columns = mesh.shape["shard"]
    devices = mesh.devices
    here, beside = devices[0, 0], devices[0, 1 % columns]
    if columns > 1 and getattr(here, "coords", 0) == getattr(beside, "coords", 1):
        return 1
    return columns


def masks_of(mesh):
    columns, total = mesh.shape["shard"], mesh.size
    pair = partner_mask(mesh)
    near, *inner = [m for m in range(1, columns) if not m & pair]
    outer = [m for m in range(columns, total, columns) if not m & pair]
    return pair, near, inner, outer


def swap(rows, mask, total):
    return lax.ppermute(rows, AXES, [(i, i ^ mask) for i in range(total)])


def join_kernel(*refs):
    *blocks, out_ref = refs
    at = 0
    for block in blocks:
        rows = block.shape[0]
        out_ref[at : at + rows, :] = block[...]
        at += rows


def best_of(kept_ref, own_ref, flag_ref, queries, micro_count, own_count):
    count = queries.shape[0]
    contract = (((1,), (1,)), ((), ()))
    block = micro_count * own_count
    cross = lax.dot_general(own_ref[...], queries, contract, preferred_element_type=jnp.float32)
    row = lax.broadcasted_iota(jnp.int32, (block, count), 0)
    column = lax.broadcasted_iota(jnp.int32, (block, count), 1)
    earlier = row // own_count < (column % block) // own_count
    usable = earlier & (flag_column(flag_ref) == 1)
    cross = jnp.where(usable, cross, NONE_YET)
    best = jnp.max(cross.reshape(block // 8, 8, count), axis=0)
    tile = min(512, kept_ref.shape[0])
    for start in range(0, kept_ref.shape[0], tile):
        scores = lax.dot_general(
            kept_ref[start : start + tile, :], queries, contract, preferred_element_type=jnp.float32
        )
        best = jnp.maximum(best, jnp.max(scores.reshape(tile // 8, 8, count), axis=0))
    return jnp.max(best, axis=0, keepdims=True)


def flag_column(flag_ref):
    groups, count = flag_ref.shape
    row = lax.broadcasted_iota(jnp.int32, (count, count), 0)
    diagonal = row == lax.broadcasted_iota(jnp.int32, (count, count), 1)
    columns = []
    for n in range(groups):
        spread = jnp.broadcast_to(flag_ref[n : n + 1, :], (count, count))
        columns.append(jnp.sum(jnp.where(diagonal, spread, 0), axis=1, keepdims=True))
    return jnp.concatenate(columns, axis=0)


def gathered(refs, spans):
    return jnp.concatenate([r[a:b, :] for r, (a, b) in zip(refs, spans, strict=True)], axis=0)


def chunk_kernel(spans, micro_count, own_count, kept_ref, own_ref, flag_ref, *refs):
    parts = len(spans)
    queries = gathered(refs[:parts], spans)
    refs[parts][...] = best_of(kept_ref, own_ref, flag_ref, queries, micro_count, own_count)


def last_kernel(spans, masks, micro_count, own_count, kept_ref, own_ref, flag_ref, *refs):
    parts = len(spans)
    queries = gathered(refs[:parts], spans)
    *earlier, out_ref = refs[parts:]
    block = micro_count * own_count
    me = lax.axis_index(AXES[0]) * lax.axis_size(AXES[1]) + lax.axis_index(AXES[1])

    def place(best, owners):
        short = -best.shape[1] % LANES
        if short:
            best = jnp.concatenate([best, jnp.zeros((1, short), best.dtype)], axis=1)
        for at, mask in enumerate(owners):
            start = at * block
            base = start // LANES * LANES
            piece = best[:, base : base + LANES]
            if start - base:
                piece = pltpu.roll(piece, LANES - (start - base), 1)
            out_ref[jnp.bitwise_xor(me, mask)] = piece

    for ref, owners in zip(earlier, masks[:-1], strict=True):
        place(ref[...], owners)
    place(best_of(kept_ref, own_ref, flag_ref, queries, micro_count, own_count), masks[-1])


def pack(pieces, block):
    room = CHUNK_ROWS // block
    chunks, spans, owners = [], [], []
    for array, masks in pieces:
        at = 0
        while at < len(masks):
            take = min(room - len(owners), len(masks) - at)
            spans.append((array, at * block, (at + take) * block))
            owners += masks[at : at + take]
            at += take
            if len(owners) == room:
                chunks.append((spans, owners))
                spans, owners = [], []
    if owners:
        chunks.append((spans, owners))
    return chunks


def per_device(mesh, kept_slab, new_rows, append_mask):
    micro_count, own_count, width = new_rows.shape
    block = micro_count * own_count
    total = mesh.size
    pair, near, inner, outer = masks_of(mesh)
    own = new_rows.reshape(block, width)
    slab_rows = kept_slab.shape[0]
    vmem = pl.BlockSpec(memory_space=pltpu.VMEM)
    small = pltpu.CompilerParams(vmem_limit_bytes=8 * 2**20)
    large = pltpu.CompilerParams(vmem_limit_bytes=24 * 2**20)

    def join(*blocks):
        rows = sum(b.shape[0] for b in blocks)
        return pl.pallas_call(
            join_kernel,
            out_shape=jax.ShapeDtypeStruct((rows, width), own.dtype),
            in_specs=[vmem] * len(blocks),
            out_specs=vmem,
            compiler_params=small,
            cost_estimate=pl.CostEstimate(
                flops=JOIN_FLOPS, bytes_accessed=4 * rows * width, transcendentals=0
            ),
        )(*blocks)

    def chunk(spans, owners, bests=(), masks=()):
        rows = len(owners) * block
        cuts = [(a, b) for _, a, b in spans]
        best = jax.ShapeDtypeStruct((1, rows), jnp.float32)
        if masks:
            body = functools.partial(last_kernel, cuts, masks)
            out = jax.ShapeDtypeStruct((total, 1, LANES), jnp.float32)
        else:
            body, out = functools.partial(chunk_kernel, cuts), best
        return pl.pallas_call(
            functools.partial(body, micro_count, own_count),
            out_shape=out,
            in_specs=[vmem] * (3 + len(spans) + len(bests)),
            out_specs=vmem,
            compiler_params=large,
            cost_estimate=pl.CostEstimate(
                flops=2 * rows * slab_rows * width,
                bytes_accessed=2 * slab_rows * width,
                transcendentals=0,
            ),
        )(kept_slab, own, append_mask, *[s[0] for s in spans], *bests)

    z = [swap(own, m, total) for m in inner]
    p = [swap(own, m, total) for m in outer]
    line = join(*z)
    far = [swap(line, m, total) for m in outer]
    side = join(own, *p[:-1])
    beside = [swap(side, near, total), swap(p[-1], near, total)]
    first = join(side, p[-1], line, far[0])
    first_pair = swap(first, pair, total)
    rest = join(*far[1:], *beside)
    rest_pair = swap(rest, pair, total)

    planes = [0, *outer]
    far_masks = [[o ^ i for i in inner] for o in outer]
    first_masks = planes + inner + far_masks[0]
    rest_masks = sum(far_masks[1:], []) + [near ^ m for m in planes]
    pieces = [(first, first_masks), (first_pair, [m ^ pair for m in first_masks])]
    pieces += [(rest, rest_masks), (rest_pair, [m ^ pair for m in rest_masks])]
    chunks = pack(pieces, block)
    bests = [chunk(*c) for c in chunks[:-1]]
    partial = chunk(*chunks[-1], bests, [owners for _, owners in chunks])
    received = lax.all_to_all(partial, AXES, split_axis=0, concat_axis=0, tiled=True)
    return jnp.max(received[:, 0, :block], axis=0).reshape(micro_count, own_count)


def solution(mesh):
    def body(kept_slab, new_rows, append_mask):
        return per_device(mesh, kept_slab, new_rows, append_mask)

    return jax.shard_map(
        body,
        mesh=mesh,
        in_specs=(
            P(AXES, None),
            P(None, AXES, None),
            P(None, AXES),
        ),
        out_specs=P(None, AXES),
        check_vma=False,
    )
```

profile of v0, /device:TPU:0, one launch (start us, length us, event | category | flops | bytes accessed | tf_op | source)
XLA Modules:
  0.0 39.8 jit_solution(4748765061627810307)
XLA Ops:
  0.0 5.1 %collective-permute-start.1 = (bf16[32,768]{1,0:T(8,128)(2,1)}, bf16[32,768]{1,0:T(8,128)(2,1)S(1)}, u32[]{:S(2)}, u32[]{:S(2)}) collective-permute-start(bf16[32,768]{1,0:T(8,128)(2,1)} %bitcast.3), channel_id=1, source_target_pairs={{0,3},{1,2},{2,1},{3,0},{4,7},{5,6},{6,5},{7,4},{8,11},{9,10},{10,... | collective-permute-start | bytes 147464 | tf_op jit(solution)/shard_map/ppermute | solution.py:35
  5.1 0.0 collective-permute-start
  5.1 2.4 %collective-permute-start.7 = (bf16[32,768]{1,0:T(8,128)(2,1)}, bf16[32,768]{1,0:T(8,128)(2,1)S(1)}, u32[]{:S(2)}, u32[]{:S(2)}) collective-permute-start(bf16[32,768]{1,0:T(8,128)(2,1)} %bitcast.5), channel_id=1, source_target_pairs={{0,24},{1,25},{2,26},{3,27},{4,28},{5,29},{6,30},{7,31},{8,16},{9,... | collective-permute-start | bytes 147464 | tf_op jit(solution)/shard_map/ppermute | solution.py:35
  7.5 0.5 %collective-permute-start.5 = (bf16[32,768]{1,0:T(8,128)(2,1)}, bf16[32,768]{1,0:T(8,128)(2,1)S(1)}, u32[]{:S(2)}, u32[]{:S(2)}) collective-permute-start(bf16[32,768]{1,0:T(8,128)(2,1)} %bitcast.6), channel_id=1, source_target_pairs={{0,16},{1,17},{2,18},{3,19},{4,20},{5,21},{6,22},{7,23},{8,24},{9,... | collective-permute-start | bytes 147464 | tf_op jit(solution)/shard_map/ppermute | solution.py:35
  8.0 0.5 %collective-permute-start.4 = (bf16[32,768]{1,0:T(8,128)(2,1)}, bf16[32,768]{1,0:T(8,128)(2,1)S(1)}, u32[]{:S(2)}, u32[]{:S(2)}) collective-permute-start(bf16[32,768]{1,0:T(8,128)(2,1)} %bitcast.7), channel_id=1, source_target_pairs={{0,8},{1,9},{2,10},{3,11},{4,12},{5,13},{6,14},{7,15},{8,0},{9,1},... | collective-permute-start | bytes 147464 | tf_op jit(solution)/shard_map/ppermute | solution.py:35
  8.6 0.0 collective-permute-done.1.refs_1_
  8.6 1.7 %collective-permute-done.refs_0_ = bf16[32,768]{1,0:T(8,128)(2,1)S(1)} collective-permute-done((bf16[32,768]{1,0:T(8,128)(2,1)}, bf16[32,768]{1,0:T(8,128)(2,1)S(1)}, u32[]{:S(2)}, u32[]{:S(2)}) %collective-permute-start) | collective-permute-done | bytes 49184 | tf_op jit(solution)/shard_map/ppermute | solution.py:35
  10.3 1.6 %collective-permute-start.10 = (bf16[64,768]{1,0:T(8,128)(2,1)S(1)}, bf16[64,768]{1,0:T(8,128)(2,1)S(1)}, u32[]{:S(2)}, u32[]{:S(2)}) collective-permute-start(bf16[64,768]{1,0:T(8,128)(2,1)S(1)} %shard_map.37.refs_2_), channel_id=1, source_target_pairs={{0,8},{1,9},{2,10},{3,11},{4,12},{5,13},{6,14},{7,15},{8,0},{9,1},... | collective-permute-start | bytes 294920 | tf_op jit(solution)/shard_map/ppermute | solution.py:35
  11.8 1.5 %collective-permute-start.3 = (bf16[64,768]{1,0:T(8,128)(2,1)S(1)}, bf16[64,768]{1,0:T(8,128)(2,1)S(1)}, u32[]{:S(2)}, u32[]{:S(2)}) collective-permute-start(bf16[64,768]{1,0:T(8,128)(2,1)S(1)} %shard_map.37.refs_2_), channel_id=1, source_target_pairs={{0,24},{1,25},{2,26},{3,27},{4,28},{5,29},{6,30},{7,31},{8,16},{9,... | collective-permute-start | bytes 294920 | tf_op jit(solution)/shard_map/ppermute | solution.py:35
  13.3 0.0 collective-permute-done.5.refs_2_
  13.3 0.5 %collective-permute-start.2 = (bf16[64,768]{1,0:T(8,128)(2,1)S(1)}, bf16[64,768]{1,0:T(8,128)(2,1)S(1)}, u32[]{:S(2)}, u32[]{:S(2)}) collective-permute-start(bf16[64,768]{1,0:T(8,128)(2,1)S(1)} %shard_map.37.refs_2_), channel_id=1, source_target_pairs={{0,16},{1,17},{2,18},{3,19},{4,20},{5,21},{6,22},{7,23},{8,24},{9,... | collective-permute-start | bytes 294920 | tf_op jit(solution)/shard_map/ppermute | solution.py:35
  13.8 0.0 collective-permute-done.4.refs_1_
  13.9 0.1 collective-permute-start.6
  13.9 0.0 collective-permute-done.7.refs_1_
  14.0 2.0 %collective-permute-start.8 = (bf16[32,768]{1,0:T(8,128)(2,1)S(1)}, bf16[32,768]{1,0:T(8,128)(2,1)S(1)}, u32[]{:S(2)}, u32[]{:S(2)}) collective-permute-start(bf16[32,768]{1,0:T(8,128)(2,1)S(1)} %collective-permute-done.7.refs_1_), channel_id=1, source_target_pairs={{0,1},{1,0},{2,3},{3,2},{4,5},{5,4},{6,7},{7,6},{8,9},{9,8},{10,11... | collective-permute-start | bytes 147464 | tf_op jit(solution)/shard_map/ppermute | solution.py:35
  16.0 0.0 collective-permute-done.10.refs_3_
  16.0 0.0 slice-start.1
  16.0 0.0 copy-start.1
  16.0 0.1 collective-permute-start.11
  16.1 3.5 %collective-permute-done.8.refs_3_ = bf16[32,768]{1,0:T(8,128)(2,1)S(1)} collective-permute-done((bf16[32,768]{1,0:T(8,128)(2,1)S(1)}, bf16[32,768]{1,0:T(8,128)(2,1)S(1)}, u32[]{:S(2)}, u32[]{:S(2)}) %collective-permute-start.8) | collective-permute-done | bytes 49184 | tf_op jit(solution)/shard_map/ppermute | solution.py:35
  19.6 0.0 collective-permute-done.3.refs_1_
  19.6 0.0 collective-permute-done.2.refs_0_
  19.6 0.0 collective-permute-done.6.refs_2_
  19.7 0.1 collective-permute-start.9
  19.8 1.9 %shard_map.41.refs_1_ = f32[1,256]{1,0:T(1,128)S(1)} custom-call(bf16[4096,768]{1,0:T(8,128)(2,1)S(1)} %bitcast.2, bf16[32,768]{1,0:T(8,128)(2,1)S(1)} %bitcast.9, s32[4,8]{1,0:T(4,128)S(1)} %copy-done.1, bf16[256,768]{1,0:T(8,128)(2,1)S(1)} %shard_map.40.refs_0_), custom_call_target="tpu_custom_call" | custom-call | flops 1610612736 | bytes 6291456 | tf_op jit(solution)/shard_map/pallas_call | solution.py:163
  21.7 1.9 %shard_map.43.refs_3_ = f32[1,256]{1,0:T(1,128)S(1)} custom-call(bf16[4096,768]{1,0:T(8,128)(2,1)S(1)} %bitcast.2, bf16[32,768]{1,0:T(8,128)(2,1)S(1)} %bitcast.10, s32[4,8]{1,0:T(4,128)S(1)} %copy-done.1, bf16[256,768]{1,0:T(8,128)(2,1)S(1)} %shard_map.39.refs_0_), custom_call_target="tpu_custom_call" | custom-call | flops 1610612736 | bytes 6291456 | tf_op jit(solution)/shard_map/pallas_call | solution.py:163
  23.7 1.9 %shard_map.42.refs_2_ = f32[1,256]{1,0:T(1,128)S(1)} custom-call(bf16[4096,768]{1,0:T(8,128)(2,1)S(1)} %bitcast.2, bf16[32,768]{1,0:T(8,128)(2,1)S(1)} %bitcast.11, s32[4,8]{1,0:T(4,128)S(1)} %copy-done.1, bf16[256,768]{1,0:T(8,128)(2,1)S(1)} %collective-permute-done.11.refs_0_), custom_call_target="tpu_custom_call" | custom-call | flops 1610612736 | bytes 6291456 | tf_op jit(solution)/shard_map/pallas_call | solution.py:163
  25.6 0.0 collective-permute-done.9.refs_0_
  25.6 2.0 %shard_map.44 = f32[32,1,128]{2,1,0:T(1,128)S(1)} custom-call(bf16[4096,768]{1,0:T(8,128)(2,1)S(1)} %bitcast.2, bf16[32,768]{1,0:T(8,128)(2,1)S(1)} %bitcast.12, s32[4,8]{1,0:T(4,128)S(1)} %copy-done.1, bf16[256,768]{1,0:T(8,128)(2,1)S(1)} %collective-permute-done.9.refs_0_, f32[1,256]{1,0:T(1,128)S(1)} %shard_map.41.refs_1_, ...), custom_call_target="tpu_custom_call" | custom-call | flops 1610612736 | bytes 6291456 | tf_op jit(solution)/shard_map/pallas_call | solution.py:163
  27.6 11.4 %all_to_all.5 = f32[32,1,128]{2,1,0:T(1,128)S(1)} all-to-all(f32[32,1,128]{2,1,0:T(1,128)S(1)} %shard_map.44), channel_id=1, replica_groups=mesh['section'=8,'shard'=4] {'section','shard'}, dimensions={0} | all-to-all | bytes 32768 | tf_op jit(solution)/shard_map/all_to_all | solution.py:196
  39.0 0.1 slice_reduce_fusion
  39.1 0.7 %reshape.7 = f32[4,8]{1,0:T(4,128)} reshape(f32[32]{0:T(128)S(1)} %slice_reduce_fusion) | data formatting | bytes 256 | tf_op jit(solution)/shard_map/reshape | solution.py:197
  (12 shorter events, 0.1 us)
Async XLA Ops:
  0.0 13.9 %copy-start = (bf16[4,8,768]{2,1,0:T(8,128)(2,1)S(1)}, bf16[4,8,768]{2,1,0:T(8,128)(2,1)}, u32[]{:S(2)}) copy-start(bf16[4,8,768]{2,1,0:T(8,128)(2,1)} %param.4) | copy-start | bytes 147460
  0.0 8.6 %collective-permute-start.1 = (bf16[32,768]{1,0:T(8,128)(2,1)}, bf16[32,768]{1,0:T(8,128)(2,1)S(1)}, u32[]{:S(2)}, u32[]{:S(2)}) collective-permute-start(bf16[32,768]{1,0:T(8,128)(2,1)} %bitcast.3), channel_id=1, source_target_pairs={{0,3},{1,2},{2,1},{3,0},{4,7},{5,6},{6,5},{7,4},{8,11},{9,10},{10,... | collective-permute-start | bytes 147464 | tf_op jit(solution)/shard_map/ppermute | solution.py:35
  5.1 5.2 %collective-permute-start = (bf16[32,768]{1,0:T(8,128)(2,1)}, bf16[32,768]{1,0:T(8,128)(2,1)S(1)}, u32[]{:S(2)}, u32[]{:S(2)}) collective-permute-start(bf16[32,768]{1,0:T(8,128)(2,1)} %bitcast.4), channel_id=1, source_target_pairs={{0,2},{1,3},{2,0},{3,1},{4,6},{5,7},{6,4},{7,5},{8,10},{9,11},{10,... | collective-permute-start | bytes 147464 | tf_op jit(solution)/shard_map/ppermute | solution.py:35
  5.1 8.9 %collective-permute-start.7 = (bf16[32,768]{1,0:T(8,128)(2,1)}, bf16[32,768]{1,0:T(8,128)(2,1)S(1)}, u32[]{:S(2)}, u32[]{:S(2)}) collective-permute-start(bf16[32,768]{1,0:T(8,128)(2,1)} %bitcast.5), channel_id=1, source_target_pairs={{0,24},{1,25},{2,26},{3,27},{4,28},{5,29},{6,30},{7,31},{8,16},{9,... | collective-permute-start | bytes 147464 | tf_op jit(solution)/shard_map/ppermute | solution.py:35
  7.5 5.8 %collective-permute-start.5 = (bf16[32,768]{1,0:T(8,128)(2,1)}, bf16[32,768]{1,0:T(8,128)(2,1)S(1)}, u32[]{:S(2)}, u32[]{:S(2)}) collective-permute-start(bf16[32,768]{1,0:T(8,128)(2,1)} %bitcast.6), channel_id=1, source_target_pairs={{0,16},{1,17},{2,18},{3,19},{4,20},{5,21},{6,22},{7,23},{8,24},{9,... | collective-permute-start | bytes 147464 | tf_op jit(solution)/shard_map/ppermute | solution.py:35
  8.0 5.8 %collective-permute-start.4 = (bf16[32,768]{1,0:T(8,128)(2,1)}, bf16[32,768]{1,0:T(8,128)(2,1)S(1)}, u32[]{:S(2)}, u32[]{:S(2)}) collective-permute-start(bf16[32,768]{1,0:T(8,128)(2,1)} %bitcast.7), channel_id=1, source_target_pairs={{0,8},{1,9},{2,10},{3,11},{4,12},{5,13},{6,14},{7,15},{8,0},{9,1},... | collective-permute-start | bytes 147464 | tf_op jit(solution)/shard_map/ppermute | solution.py:35
  10.3 5.7 %collective-permute-start.10 = (bf16[64,768]{1,0:T(8,128)(2,1)S(1)}, bf16[64,768]{1,0:T(8,128)(2,1)S(1)}, u32[]{:S(2)}, u32[]{:S(2)}) collective-permute-start(bf16[64,768]{1,0:T(8,128)(2,1)S(1)} %shard_map.37.refs_2_), channel_id=1, source_target_pairs={{0,8},{1,9},{2,10},{3,11},{4,12},{5,13},{6,14},{7,15},{8,0},{9,1},... | collective-permute-start | bytes 294920 | tf_op jit(solution)/shard_map/ppermute | solution.py:35
  11.8 7.8 %collective-permute-start.3 = (bf16[64,768]{1,0:T(8,128)(2,1)S(1)}, bf16[64,768]{1,0:T(8,128)(2,1)S(1)}, u32[]{:S(2)}, u32[]{:S(2)}) collective-permute-start(bf16[64,768]{1,0:T(8,128)(2,1)S(1)} %shard_map.37.refs_2_), channel_id=1, source_target_pairs={{0,24},{1,25},{2,26},{3,27},{4,28},{5,29},{6,30},{7,31},{8,16},{9,... | collective-permute-start | bytes 294920 | tf_op jit(solution)/shard_map/ppermute | solution.py:35
  13.3 6.3 %collective-permute-start.2 = (bf16[64,768]{1,0:T(8,128)(2,1)S(1)}, bf16[64,768]{1,0:T(8,128)(2,1)S(1)}, u32[]{:S(2)}, u32[]{:S(2)}) collective-permute-start(bf16[64,768]{1,0:T(8,128)(2,1)S(1)} %shard_map.37.refs_2_), channel_id=1, source_target_pairs={{0,16},{1,17},{2,18},{3,19},{4,20},{5,21},{6,22},{7,23},{8,24},{9,... | collective-permute-start | bytes 294920 | tf_op jit(solution)/shard_map/ppermute | solution.py:35
  13.9 5.7 %collective-permute-start.6 = (bf16[96,768]{1,0:T(8,128)(2,1)S(1)}, bf16[96,768]{1,0:T(8,128)(2,1)S(1)}, u32[]{:S(2)}, u32[]{:S(2)}) collective-permute-start(bf16[96,768]{1,0:T(8,128)(2,1)S(1)} %shard_map.38.refs_0_), channel_id=1, source_target_pairs={{0,1},{1,0},{2,3},{3,2},{4,5},{5,4},{6,7},{7,6},{8,9},{9,8},{10,11... | collective-permute-start | bytes 442376 | tf_op jit(solution)/shard_map/ppermute | solution.py:35
  14.0 5.6 %collective-permute-start.8 = (bf16[32,768]{1,0:T(8,128)(2,1)S(1)}, bf16[32,768]{1,0:T(8,128)(2,1)S(1)}, u32[]{:S(2)}, u32[]{:S(2)}) collective-permute-start(bf16[32,768]{1,0:T(8,128)(2,1)S(1)} %collective-permute-done.7.refs_1_), channel_id=1, source_target_pairs={{0,1},{1,0},{2,3},{3,2},{4,5},{5,4},{6,7},{7,6},{8,9},{9,8},{10,11... | collective-permute-start | bytes 147464 | tf_op jit(solution)/shard_map/ppermute | solution.py:35
  16.0 3.8 %slice-start = ((s8[6291456]{0:T(1024)(128)(4,1)}), s8[4194304]{0:T(1024)(128)(4,1)S(1)}, s32[]{:S(2)}) async-start(s8[6291456]{0:T(1024)(128)(4,1)} %bitcast.1), calls=%async_computation.1 | async-start | bytes 8388608
  16.0 3.7 %slice-start.1 = ((s8[6291456]{0:T(1024)(128)(4,1)}), s8[2097152]{0:T(1024)(128)(4,1)S(1)}, s32[]{:S(2)}) async-start(s8[6291456]{0:T(1024)(128)(4,1)} %bitcast.1), calls=%async_computation.2 | async-start | bytes 4194304
  16.0 3.7 %copy-start.1 = (s32[4,8]{1,0:T(4,128)S(1)}, s32[4,8]{1,0:T(4,128)}, u32[]{:S(2)}) copy-start(s32[4,8]{1,0:T(4,128)} %flag_ref.7) | copy-start | bytes 388
  16.0 7.6 %collective-permute-start.11 = (bf16[256,768]{1,0:T(8,128)(2,1)S(1)}, bf16[256,768]{1,0:T(8,128)(2,1)S(1)}, u32[]{:S(2)}, u32[]{:S(2)}) collective-permute-start(bf16[256,768]{1,0:T(8,128)(2,1)S(1)} %shard_map.40.refs_0_), channel_id=1, source_target_pairs={{0,4},{1,5},{2,6},{3,7},{4,0},{5,1},{6,2},{7,3},{8,12},{9,13},{10,... | collective-permute-start | bytes 1179656 | tf_op jit(solution)/shard_map/ppermute | solution.py:35
  19.7 6.0 %collective-permute-start.9 = (bf16[256,768]{1,0:T(8,128)(2,1)S(1)}, bf16[256,768]{1,0:T(8,128)(2,1)S(1)}, u32[]{:S(2)}, u32[]{:S(2)}) collective-permute-start(bf16[256,768]{1,0:T(8,128)(2,1)S(1)} %shard_map.39.refs_0_), channel_id=1, source_target_pairs={{0,4},{1,5},{2,6},{3,7},{4,0},{5,1},{6,2},{7,3},{8,12},{9,13},{10,... | collective-permute-start | bytes 1179656 | tf_op jit(solution)/shard_map/ppermute | solution.py:35
where the time goes:
time: 39.9 us; the launch traced here: 39.8 us
  starting transfers between devices  14.3 us (36%)
  blocking collectives  11.4 us (29%)
  Pallas kernels  7.89 us (20%)
  waiting for transfers between devices  5.23 us (13%)
  local copies, waits for them, and re-layouts  0.68 us (2%)
    ppermute x12, starting transfers between devices, swap(): return lax.ppermute(rows, AXES, [(i, i ^ mask) for i in range(total)])  14.3 us
    all_to_all x1, blocking collectives, per_device(): lax.all_to_all(partial, AXES, split_axis=0, concat_axis=0, tiled=True)  11.4 us
    pallas_call x4, Pallas kernels, chunk(): pl.pallas_call(functools.partial(body, micro_count, own_count), out_shape...  7.82 us
    ppermute x12, waiting for transfers between devices, swap(): return lax.ppermute(rows, AXES, [(i, i ^ mask) for i in range(total)])  5.23 us
  transfers between devices with their start and end apart: 12, of which 2 were waited for; matrix products, arithmetic and copies ran while one was open for 0% of the time, Pallas kernels for 15%

commit v1 on v0

--- a/solution.py
+++ b/solution.py
@@ -31,8 +31,17 @@
     return pair, near, inner, outer
 
 
-def swap(rows, mask, total):
-    return lax.ppermute(rows, AXES, [(i, i ^ mask) for i in range(total)])
+def swap(rows, mask, total, pair=0, other=None):
+    second = mask if other is None else other
+    return lax.ppermute(rows, AXES, [(i, i ^ (second if i & pair else mask)) for i in range(total)])
+
+
+def twin_kernel(own_ref, other_ref, out_ref, sem):
+    rows = own_ref.shape[0]
+    copy = pltpu.make_async_copy(own_ref, out_ref.at[pl.ds(0, rows)], sem)
+    copy.start()
+    out_ref[rows : 2 * rows, :] = other_ref[...]
+    copy.wait()
 
 
 def join_kernel(*refs):
@@ -55,7 +64,7 @@
     usable = earlier & (flag_column(flag_ref) == 1)
     cross = jnp.where(usable, cross, NONE_YET)
     best = jnp.max(cross.reshape(block // 8, 8, count), axis=0)
-    tile = min(512, kept_ref.shape[0])
+    tile = kept_ref.shape[0]
     for start in range(0, kept_ref.shape[0], tile):
         scores = lax.dot_general(
             kept_ref[start : start + tile, :], queries, contract, preferred_element_type=jnp.float32
@@ -85,23 +94,26 @@
     refs[parts][...] = best_of(kept_ref, own_ref, flag_ref, queries, micro_count, own_count)
 
 
-def last_kernel(spans, masks, micro_count, own_count, kept_ref, own_ref, flag_ref, *refs):
+def last_kernel(spans, masks, pair, micro_count, own_count, kept_ref, own_ref, flag_ref, *refs):
     parts = len(spans)
     queries = gathered(refs[:parts], spans)
     *earlier, out_ref = refs[parts:]
     block = micro_count * own_count
     me = lax.axis_index(AXES[0]) * lax.axis_size(AXES[1]) + lax.axis_index(AXES[1])
+    second = jnp.bitwise_and(me, pair) != 0
 
     def place(best, owners):
         short = -best.shape[1] % LANES
         if short:
             best = jnp.concatenate([best, jnp.zeros((1, short), best.dtype)], axis=1)
-        for at, mask in enumerate(owners):
+        for at, (mask, other) in enumerate(owners):
             start = at * block
             base = start // LANES * LANES
             piece = best[:, base : base + LANES]
             if start - base:
                 piece = pltpu.roll(piece, LANES - (start - base), 1)
+            if other != mask:
+                mask = jnp.where(second, other, mask)
             out_ref[jnp.bitwise_xor(me, mask)] = piece
 
     for ref, owners in zip(earlier, masks[:-1], strict=True):
@@ -156,7 +168,7 @@
         cuts = [(a, b) for _, a, b in spans]
         best = jax.ShapeDtypeStruct((1, rows), jnp.float32)
         if masks:
-            body = functools.partial(last_kernel, cuts, masks)
+            body = functools.partial(last_kernel, cuts, masks, pair)
             out = jax.ShapeDtypeStruct((total, 1, LANES), jnp.float32)
         else:
             body, out = functools.partial(chunk_kernel, cuts), best
@@ -173,23 +185,35 @@
             ),
         )(kept_slab, own, append_mask, *[s[0] for s in spans], *bests)
 
+    own_pair = swap(own, pair, total)
     z = [swap(own, m, total) for m in inner]
-    p = [swap(own, m, total) for m in outer]
+    twins = pl.pallas_call(
+        twin_kernel,
+        out_shape=jax.ShapeDtypeStruct((2 * block, width), own.dtype),
+        in_specs=[pl.BlockSpec(memory_space=pltpu.HBM), vmem],
+        out_specs=vmem,
+        scratch_shapes=[pltpu.SemaphoreType.DMA(())],
+        compiler_params=small,
+    )(pltpu.with_memory_space_constraint(own, pltpu.HBM), own_pair)
+    p = [swap(twins, outer[0], total, pair, outer[1])]
+    p += [swap(own, m, total) for m in outer[2:]]
     line = join(*z)
     far = [swap(line, m, total) for m in outer]
-    side = join(own, *p[:-1])
-    beside = [swap(side, near, total), swap(p[-1], near, total)]
-    first = join(side, p[-1], line, far[0])
+    side = join(own, *p)
+    beside = swap(side, near, total)
+    first = join(side, line, far[0])
     first_pair = swap(first, pair, total)
-    rest = join(*far[1:], *beside)
+    rest = join(*far[1:], beside)
     rest_pair = swap(rest, pair, total)
 
-    planes = [0, *outer]
-    far_masks = [[o ^ i for i in inner] for o in outer]
-    first_masks = planes + inner + far_masks[0]
-    rest_masks = sum(far_masks[1:], []) + [near ^ m for m in planes]
-    pieces = [(first, first_masks), (first_pair, [m ^ pair for m in first_masks])]
-    pieces += [(rest, rest_masks), (rest_pair, [m ^ pair for m in rest_masks])]
+    both = lambda masks: [(m, m) for m in masks]
+    across = lambda masks: [(b ^ pair, a ^ pair) for a, b in masks]
+    planes = [(0, 0), (outer[0], outer[1]), (outer[0] ^ pair, outer[1] ^ pair), *both(outer[2:])]
+    far_masks = [both([o ^ i for i in inner]) for o in outer]
+    first_masks = planes + both(inner) + far_masks[0]
+    rest_masks = sum(far_masks[1:], []) + [(a ^ near, b ^ near) for a, b in planes]
+    pieces = [(first, first_masks), (first_pair, across(first_masks))]
+    pieces += [(rest, rest_masks), (rest_pair, across(rest_masks))]
     chunks = pack(pieces, block)
     bests = [chunk(*c) for c in chunks[:-1]]
     partial = chunk(*chunks[-1], bests, [owners for _, owners in chunks])

time: 39.9 us -> 40.2 us (level)
  starting transfers between devices: 14.3 us -> 12.2 us
  waiting for transfers between devices: 5.23 us -> 6.56 us
  Pallas kernels: 7.89 us -> 8.76 us
    ppermute x12 -> x11, starting transfers between devices: 14.3 us -> 12.2 us  [swap(): lax.ppermute(rows, AXES, [(i, i ^ (second if i & pair else mask)) for i i...]
    ppermute x12 -> x11, waiting for transfers between devices: 5.23 us -> 6.56 us  [swap(): lax.ppermute(rows, AXES, [(i, i ^ (second if i & pair else mask)) for i i...]
    pallas_call x0 -> x1, Pallas kernels: none -> 0.84 us  [per_device(): pl.pallas_call(twin_kernel, out_shape=jax.ShapeDtypeStruct((2 * block, wi...]
  transfers between devices with their start and end apart: 12 -> 11, of which waited for: 2 -> 5; matrix products, arithmetic and copies ran while one was open for 0% -> 0% of each run, Pallas kernels for 15% -> 17%
where the time goes in v1:
time: 40.2 us; the launch traced here: 40 us
  starting transfers between devices  12.2 us (30%)
  blocking collectives  11.6 us (29%)
  Pallas kernels  8.76 us (22%)
  waiting for transfers between devices  6.56 us (16%)
  local copies, waits for them, and re-layouts  0.69 us (2%)
    ppermute x11, starting transfers between devices, swap(): lax.ppermute(rows, AXES, [(i, i ^ (second if i & pair else mask)) for i i...  12.2 us
    all_to_all x1, blocking collectives, per_device(): lax.all_to_all(partial, AXES, split_axis=0, concat_axis=0, tiled=True)  11.6 us
    pallas_call x4, Pallas kernels, chunk(): pl.pallas_call(functools.partial(body, micro_count, own_count), out_shape...  7.84 us
    ppermute x11, waiting for transfers between devices, swap(): lax.ppermute(rows, AXES, [(i, i ^ (second if i & pair else mask)) for i i...  6.56 us
    pallas_call x1, Pallas kernels, per_device(): pl.pallas_call(twin_kernel, out_shape=jax.ShapeDtypeStruct((2 * block, wi...  0.84 us
  transfers between devices with their start and end apart: 11, of which 5 were waited for; matrix products, arithmetic and copies ran while one was open for 0% of the time, Pallas kernels for 17%

profile of v1, /device:TPU:0, one launch (start us, length us, event | category | flops | bytes accessed | tf_op | source)
XLA Modules:
  0.0 40.0 jit_solution(17222557656428089454)
XLA Ops:
  0.0 0.5 %collective-permute-start.4 = (bf16[32,768]{1,0:T(8,128)(2,1)}, bf16[32,768]{1,0:T(8,128)(2,1)S(1)}, u32[]{:S(2)}, u32[]{:S(2)}) collective-permute-start(bf16[32,768]{1,0:T(8,128)(2,1)} %bitcast.3), channel_id=1, source_target_pairs={{0,4},{1,5},{2,6},{3,7},{4,0},{5,1},{6,2},{7,3},{8,12},{9,13},{10,... | collective-permute-start | bytes 147464 | tf_op jit(solution)/shard_map/ppermute | solution.py:36
  0.5 4.6 %collective-permute-start.1 = (bf16[32,768]{1,0:T(8,128)(2,1)}, bf16[32,768]{1,0:T(8,128)(2,1)S(1)}, u32[]{:S(2)}, u32[]{:S(2)}) collective-permute-start(bf16[32,768]{1,0:T(8,128)(2,1)} %bitcast.4), channel_id=1, source_target_pairs={{0,3},{1,2},{2,1},{3,0},{4,7},{5,6},{6,5},{7,4},{8,11},{9,10},{10,... | collective-permute-start | bytes 147464 | tf_op jit(solution)/shard_map/ppermute | solution.py:36
  5.1 0.0 collective-permute-start
  5.1 2.4 %collective-permute-start.6 = (bf16[32,768]{1,0:T(8,128)(2,1)}, bf16[32,768]{1,0:T(8,128)(2,1)S(1)}, u32[]{:S(2)}, u32[]{:S(2)}) collective-permute-start(bf16[32,768]{1,0:T(8,128)(2,1)} %bitcast.6), channel_id=1, source_target_pairs={{0,24},{1,25},{2,26},{3,27},{4,28},{5,29},{6,30},{7,31},{8,16},{9,... | collective-permute-start | bytes 147464 | tf_op jit(solution)/shard_map/ppermute | solution.py:36
  7.5 0.0 collective-permute-done.4.other_ref
  7.5 0.8 %shard_map.38 = bf16[64,768]{1,0:T(8,128)(2,1)S(1)} custom-call(bf16[32,768]{1,0:T(8,128)(2,1)} %bitcast.7, bf16[32,768]{1,0:T(8,128)(2,1)S(1)} %collective-permute-done.4.other_ref), custom_call_target="tpu_custom_call" | custom-call | tf_op jit(solution)/shard_map/pallas_call | solution.py:190
  8.4 0.0 copy-start
  8.4 0.6 %collective-permute-start.5 = (bf16[64,768]{1,0:T(8,128)(2,1)S(1)}, bf16[64,768]{1,0:T(8,128)(2,1)S(1)}, u32[]{:S(2)}, u32[]{:S(2)}) collective-permute-start(bf16[64,768]{1,0:T(8,128)(2,1)S(1)} %shard_map.38), channel_id=1, source_target_pairs={{0,8},{1,9},{2,10},{3,11},{4,20},{5,21},{6,22},{7,23},{8,0},{9,1},... | collective-permute-start | bytes 294920 | tf_op jit(solution)/shard_map/ppermute | solution.py:36
  9.0 0.0 collective-permute-done.1.refs_1_
  9.0 1.3 %collective-permute-done.refs_0_ = bf16[32,768]{1,0:T(8,128)(2,1)S(1)} collective-permute-done((bf16[32,768]{1,0:T(8,128)(2,1)}, bf16[32,768]{1,0:T(8,128)(2,1)S(1)}, u32[]{:S(2)}, u32[]{:S(2)}) %collective-permute-start) | collective-permute-done | bytes 49184 | tf_op jit(solution)/shard_map/ppermute | solution.py:36
  10.3 1.6 %collective-permute-start.9 = (bf16[64,768]{1,0:T(8,128)(2,1)S(1)}, bf16[64,768]{1,0:T(8,128)(2,1)S(1)}, u32[]{:S(2)}, u32[]{:S(2)}) collective-permute-start(bf16[64,768]{1,0:T(8,128)(2,1)S(1)} %shard_map.37.refs_1_), channel_id=1, source_target_pairs={{0,8},{1,9},{2,10},{3,11},{4,12},{5,13},{6,14},{7,15},{8,0},{9,1},... | collective-permute-start | bytes 294920 | tf_op jit(solution)/shard_map/ppermute | solution.py:36
  11.9 1.5 %collective-permute-start.3 = (bf16[64,768]{1,0:T(8,128)(2,1)S(1)}, bf16[64,768]{1,0:T(8,128)(2,1)S(1)}, u32[]{:S(2)}, u32[]{:S(2)}) collective-permute-start(bf16[64,768]{1,0:T(8,128)(2,1)S(1)} %shard_map.37.refs_1_), channel_id=1, source_target_pairs={{0,24},{1,25},{2,26},{3,27},{4,28},{5,29},{6,30},{7,31},{8,16},{9,... | collective-permute-start | bytes 294920 | tf_op jit(solution)/shard_map/ppermute | solution.py:36
  13.4 0.5 %collective-permute-start.2 = (bf16[64,768]{1,0:T(8,128)(2,1)S(1)}, bf16[64,768]{1,0:T(8,128)(2,1)S(1)}, u32[]{:S(2)}, u32[]{:S(2)}) collective-permute-start(bf16[64,768]{1,0:T(8,128)(2,1)S(1)} %shard_map.37.refs_1_), channel_id=1, source_target_pairs={{0,16},{1,17},{2,18},{3,19},{4,20},{5,21},{6,22},{7,23},{8,24},{9,... | collective-permute-start | bytes 294920 | tf_op jit(solution)/shard_map/ppermute | solution.py:36
  13.9 0.0 collective-permute-done.6.refs_2_
  13.9 0.0 collective-permute-done.5.refs_1_
  13.9 0.4 collective-permute-start.7
  14.3 1.3 %collective-permute-done.9.refs_2_ = bf16[64,768]{1,0:T(8,128)(2,1)S(1)} collective-permute-done((bf16[64,768]{1,0:T(8,128)(2,1)S(1)}, bf16[64,768]{1,0:T(8,128)(2,1)S(1)}, u32[]{:S(2)}, u32[]{:S(2)}) %collective-permute-start.9) | collective-permute-done | bytes 98336 | tf_op jit(solution)/shard_map/ppermute | solution.py:36
  15.6 0.0 slice-start.1
  15.6 0.0 copy-start.1
  15.6 0.1 collective-permute-start.10
  15.7 2.3 %collective-permute-done.3.refs_1_ = bf16[64,768]{1,0:T(8,128)(2,1)S(1)} collective-permute-done((bf16[64,768]{1,0:T(8,128)(2,1)S(1)}, bf16[64,768]{1,0:T(8,128)(2,1)S(1)}, u32[]{:S(2)}, u32[]{:S(2)}) %collective-permute-start.3) | collective-permute-done | bytes 98336 | tf_op jit(solution)/shard_map/ppermute | solution.py:36
  18.0 1.0 %collective-permute-done.2.refs_0_ = bf16[64,768]{1,0:T(8,128)(2,1)S(1)} collective-permute-done((bf16[64,768]{1,0:T(8,128)(2,1)S(1)}, bf16[64,768]{1,0:T(8,128)(2,1)S(1)}, u32[]{:S(2)}, u32[]{:S(2)}) %collective-permute-start.2) | collective-permute-done | bytes 98336 | tf_op jit(solution)/shard_map/ppermute | solution.py:36
  19.0 0.7 %collective-permute-done.7.refs_2_ = bf16[128,768]{1,0:T(8,128)(2,1)S(1)} collective-permute-done((bf16[128,768]{1,0:T(8,128)(2,1)S(1)}, bf16[128,768]{1,0:T(8,128)(2,1)S(1)}, u32[]{:S(2)}, u32[]{:S(2)}) %collective-permute-start.7) | collective-permute-done | bytes 196640 | tf_op jit(solution)/shard_map/ppermute | solution.py:36
  19.7 0.1 collective-permute-start.8
  19.8 1.9 %shard_map.42.refs_1_ = f32[1,256]{1,0:T(1,128)S(1)} custom-call(bf16[4096,768]{1,0:T(8,128)(2,1)S(1)} %bitcast.2, bf16[32,768]{1,0:T(8,128)(2,1)S(1)} %bitcast.9, s32[4,8]{1,0:T(4,128)S(1)} %copy-done.1, bf16[256,768]{1,0:T(8,128)(2,1)S(1)} %shard_map.41.refs_0_), custom_call_target="tpu_custom_call" | custom-call | flops 1610612736 | bytes 6291456 | tf_op jit(solution)/shard_map/pallas_call | solution.py:175
  21.8 1.9 %shard_map.44.refs_3_ = f32[1,256]{1,0:T(1,128)S(1)} custom-call(bf16[4096,768]{1,0:T(8,128)(2,1)S(1)} %bitcast.2, bf16[32,768]{1,0:T(8,128)(2,1)S(1)} %bitcast.10, s32[4,8]{1,0:T(4,128)S(1)} %copy-done.1, bf16[256,768]{1,0:T(8,128)(2,1)S(1)} %shard_map.40.refs_0_), custom_call_target="tpu_custom_call" | custom-call | flops 1610612736 | bytes 6291456 | tf_op jit(solution)/shard_map/pallas_call | solution.py:175
  23.7 0.0 collective-permute-done.10.refs_0_
  23.7 1.9 %shard_map.43.refs_2_ = f32[1,256]{1,0:T(1,128)S(1)} custom-call(bf16[4096,768]{1,0:T(8,128)(2,1)S(1)} %bitcast.2, bf16[32,768]{1,0:T(8,128)(2,1)S(1)} %bitcast.11, s32[4,8]{1,0:T(4,128)S(1)} %copy-done.1, bf16[256,768]{1,0:T(8,128)(2,1)S(1)} %collective-permute-done.10.refs_0_), custom_call_target="tpu_custom_call" | custom-call | flops 1610612736 | bytes 6291456 | tf_op jit(solution)/shard_map/pallas_call | solution.py:175
  25.7 2.0 %shard_map.45 = f32[32,1,128]{2,1,0:T(1,128)S(1)} custom-call(bf16[4096,768]{1,0:T(8,128)(2,1)S(1)} %bitcast.2, bf16[32,768]{1,0:T(8,128)(2,1)S(1)} %bitcast.12, s32[4,8]{1,0:T(4,128)S(1)} %copy-done.1, bf16[256,768]{1,0:T(8,128)(2,1)S(1)} %collective-permute-done.8.refs_0_, f32[1,256]{1,0:T(1,128)S(1)} %shard_map.42.refs_1_, ...), custom_call_target="tpu_custom_call" | custom-call | flops 1610612736 | bytes 6291456 | tf_op jit(solution)/shard_map/pallas_call | solution.py:175
  27.7 11.6 %all_to_all.5 = f32[32,1,128]{2,1,0:T(1,128)S(1)} all-to-all(f32[32,1,128]{2,1,0:T(1,128)S(1)} %shard_map.45), channel_id=1, replica_groups=mesh['section'=8,'shard'=4] {'section','shard'}, dimensions={0} | all-to-all | bytes 32768 | tf_op jit(solution)/shard_map/all_to_all | solution.py:220
  39.3 0.1 slice_reduce_fusion
  39.4 0.7 %reshape.7 = f32[4,8]{1,0:T(4,128)} reshape(f32[32]{0:T(128)S(1)} %slice_reduce_fusion) | data formatting | bytes 256 | tf_op jit(solution)/shard_map/reshape | solution.py:221
  (11 shorter events, 0.1 us)
Async XLA Ops:
  0.0 7.5 %collective-permute-start.4 = (bf16[32,768]{1,0:T(8,128)(2,1)}, bf16[32,768]{1,0:T(8,128)(2,1)S(1)}, u32[]{:S(2)}, u32[]{:S(2)}) collective-permute-start(bf16[32,768]{1,0:T(8,128)(2,1)} %bitcast.3), channel_id=1, source_target_pairs={{0,4},{1,5},{2,6},{3,7},{4,0},{5,1},{6,2},{7,3},{8,12},{9,13},{10,... | collective-permute-start | bytes 147464 | tf_op jit(solution)/shard_map/ppermute | solution.py:36
  0.5 8.5 %collective-permute-start.1 = (bf16[32,768]{1,0:T(8,128)(2,1)}, bf16[32,768]{1,0:T(8,128)(2,1)S(1)}, u32[]{:S(2)}, u32[]{:S(2)}) collective-permute-start(bf16[32,768]{1,0:T(8,128)(2,1)} %bitcast.4), channel_id=1, source_target_pairs={{0,3},{1,2},{2,1},{3,0},{4,7},{5,6},{6,5},{7,4},{8,11},{9,10},{10,... | collective-permute-start | bytes 147464 | tf_op jit(solution)/shard_map/ppermute | solution.py:36
  5.1 5.2 %collective-permute-start = (bf16[32,768]{1,0:T(8,128)(2,1)}, bf16[32,768]{1,0:T(8,128)(2,1)S(1)}, u32[]{:S(2)}, u32[]{:S(2)}) collective-permute-start(bf16[32,768]{1,0:T(8,128)(2,1)} %bitcast.5), channel_id=1, source_target_pairs={{0,2},{1,3},{2,0},{3,1},{4,6},{5,7},{6,4},{7,5},{8,10},{9,11},{10,... | collective-permute-start | bytes 147464 | tf_op jit(solution)/shard_map/ppermute | solution.py:36
  5.1 8.8 %collective-permute-start.6 = (bf16[32,768]{1,0:T(8,128)(2,1)}, bf16[32,768]{1,0:T(8,128)(2,1)S(1)}, u32[]{:S(2)}, u32[]{:S(2)}) collective-permute-start(bf16[32,768]{1,0:T(8,128)(2,1)} %bitcast.6), channel_id=1, source_target_pairs={{0,24},{1,25},{2,26},{3,27},{4,28},{5,29},{6,30},{7,31},{8,16},{9,... | collective-permute-start | bytes 147464 | tf_op jit(solution)/shard_map/ppermute | solution.py:36
  8.4 5.5 %copy-start = (bf16[4,8,768]{2,1,0:T(8,128)(2,1)S(1)}, bf16[4,8,768]{2,1,0:T(8,128)(2,1)}, u32[]{:S(2)}) copy-start(bf16[4,8,768]{2,1,0:T(8,128)(2,1)} %param.4) | copy-start | bytes 147460
  8.4 5.5 %collective-permute-start.5 = (bf16[64,768]{1,0:T(8,128)(2,1)S(1)}, bf16[64,768]{1,0:T(8,128)(2,1)S(1)}, u32[]{:S(2)}, u32[]{:S(2)}) collective-permute-start(bf16[64,768]{1,0:T(8,128)(2,1)S(1)} %shard_map.38), channel_id=1, source_target_pairs={{0,8},{1,9},{2,10},{3,11},{4,20},{5,21},{6,22},{7,23},{8,0},{9,1},... | collective-permute-start | bytes 294920 | tf_op jit(solution)/shard_map/ppermute | solution.py:36
  10.3 5.2 %collective-permute-start.9 = (bf16[64,768]{1,0:T(8,128)(2,1)S(1)}, bf16[64,768]{1,0:T(8,128)(2,1)S(1)}, u32[]{:S(2)}, u32[]{:S(2)}) collective-permute-start(bf16[64,768]{1,0:T(8,128)(2,1)S(1)} %shard_map.37.refs_1_), channel_id=1, source_target_pairs={{0,8},{1,9},{2,10},{3,11},{4,12},{5,13},{6,14},{7,15},{8,0},{9,1},... | collective-permute-start | bytes 294920 | tf_op jit(solution)/shard_map/ppermute | solution.py:36
  11.9 6.1 %collective-permute-start.3 = (bf16[64,768]{1,0:T(8,128)(2,1)S(1)}, bf16[64,768]{1,0:T(8,128)(2,1)S(1)}, u32[]{:S(2)}, u32[]{:S(2)}) collective-permute-start(bf16[64,768]{1,0:T(8,128)(2,1)S(1)} %shard_map.37.refs_1_), channel_id=1, source_target_pairs={{0,24},{1,25},{2,26},{3,27},{4,28},{5,29},{6,30},{7,31},{8,16},{9,... | collective-permute-start | bytes 294920 | tf_op jit(solution)/shard_map/ppermute | solution.py:36
  13.4 5.6 %collective-permute-start.2 = (bf16[64,768]{1,0:T(8,128)(2,1)S(1)}, bf16[64,768]{1,0:T(8,128)(2,1)S(1)}, u32[]{:S(2)}, u32[]{:S(2)}) collective-permute-start(bf16[64,768]{1,0:T(8,128)(2,1)S(1)} %shard_map.37.refs_1_), channel_id=1, source_target_pairs={{0,16},{1,17},{2,18},{3,19},{4,20},{5,21},{6,22},{7,23},{8,24},{9,... | collective-permute-start | bytes 294920 | tf_op jit(solution)/shard_map/ppermute | solution.py:36
  13.9 5.7 %collective-permute-start.7 = (bf16[128,768]{1,0:T(8,128)(2,1)S(1)}, bf16[128,768]{1,0:T(8,128)(2,1)S(1)}, u32[]{:S(2)}, u32[]{:S(2)}) collective-permute-start(bf16[128,768]{1,0:T(8,128)(2,1)S(1)} %shard_map.39.refs_0_), channel_id=1, source_target_pairs={{0,1},{1,0},{2,3},{3,2},{4,5},{5,4},{6,7},{7,6},{8,9},{9,8},{10,11... | collective-permute-start | bytes 589832 | tf_op jit(solution)/shard_map/ppermute | solution.py:36
  15.6 4.2 %slice-start = ((s8[6291456]{0:T(1024)(128)(4,1)}), s8[4194304]{0:T(1024)(128)(4,1)S(1)}, s32[]{:S(2)}) async-start(s8[6291456]{0:T(1024)(128)(4,1)} %bitcast.1), calls=%async_computation.1 | async-start | bytes 8388608
  15.6 4.2 %slice-start.1 = ((s8[6291456]{0:T(1024)(128)(4,1)}), s8[2097152]{0:T(1024)(128)(4,1)S(1)}, s32[]{:S(2)}) async-start(s8[6291456]{0:T(1024)(128)(4,1)} %bitcast.1), calls=%async_computation.2 | async-start | bytes 4194304
  15.6 4.2 %copy-start.1 = (s32[4,8]{1,0:T(4,128)S(1)}, s32[4,8]{1,0:T(4,128)}, u32[]{:S(2)}) copy-start(s32[4,8]{1,0:T(4,128)} %flag_ref.7) | copy-start | bytes 388
  15.6 8.1 %collective-permute-start.10 = (bf16[256,768]{1,0:T(8,128)(2,1)S(1)}, bf16[256,768]{1,0:T(8,128)(2,1)S(1)}, u32[]{:S(2)}, u32[]{:S(2)}) collective-permute-start(bf16[256,768]{1,0:T(8,128)(2,1)S(1)} %shard_map.41.refs_0_), channel_id=1, source_target_pairs={{0,4},{1,5},{2,6},{3,7},{4,0},{5,1},{6,2},{7,3},{8,12},{9,13},{10,... | collective-permute-start | bytes 1179656 | tf_op jit(solution)/shard_map/ppermute | solution.py:36
  19.7 6.0 %collective-permute-start.8 = (bf16[256,768]{1,0:T(8,128)(2,1)S(1)}, bf16[256,768]{1,0:T(8,128)(2,1)S(1)}, u32[]{:S(2)}, u32[]{:S(2)}) collective-permute-start(bf16[256,768]{1,0:T(8,128)(2,1)S(1)} %shard_map.40.refs_0_), channel_id=1, source_target_pairs={{0,4},{1,5},{2,6},{3,7},{4,0},{5,1},{6,2},{7,3},{8,12},{9,13},{10,... | collective-permute-start | bytes 1179656 | tf_op jit(solution)/shard_map/ppermute | solution.py:36
